TPU v7x, 32 devices: a whole 2x2x4 slice. The times are simulated.
32 devices in a mesh: fsdp: 4 (over y, x), dp: 8 (over z, core).
Axes of the slice: x: 2, y: 2, z: 4, core: 2. Of those that a mesh axis runs over, the one named last changes fastest.
Arguments:
- tokens: bfloat16 [16384, 1152], P(('fsdp', 'dp')), may hold values from -6 to 6
- conditions: bfloat16 [64, 1152], P(('fsdp', 'dp')), may hold values from -6 to 6
- cotangent: bfloat16 [16384, 1152], P(('fsdp', 'dp')), may hold values from -6 to 6
- slot_mask: int32 [64], P(('fsdp', 'dp')), may hold values from 0 to 1, as said below
- weight_flat: bfloat16 [186624, 128], P(('fsdp', 'dp')), may hold values from -3 to 3
- bias_flat: bfloat16 [17664], P(('fsdp', 'dp')), may hold values from -2 to 2
Outputs:
- out: bfloat16 [16384, 1152], P(('fsdp', 'dp'))
- grad_tokens: float32 [16384, 1152], P(('fsdp', 'dp'))
- grad_conditions: float32 [64, 1152], P(('fsdp', 'dp'))
- grad_weights: float32 [186624, 128], P(('fsdp', 'dp'))
- grad_biases: float32 [17664], P(('fsdp', 'dp'))
Inputs may be any that keep to these rules, and one draw needn't show every extreme that they name: `slot_mask`: on each device's 2 image slots the live ones come first; a device has one live image or all 2, and some device has all 2 live in every draw.
All inputs are finite; a program needn't handle non-finite values.
Results may differ from a plain program's by a relative error of at most 0.0095.
Values may be sent and summed in bfloat16 or wider, within the bound.
No kernel may reach another device: no remote copies, remote signals or barrier semaphores. Data moves between devices by JAX's collectives and lax.ppermute only.
A program may use at most 576 MiB of HBM per device.

v0:
```python
import math
import jax
import jax.numpy as jnp
from jax import lax
from jax.sharding import PartitionSpec as P

D = 1152
HEADS = 16
HEAD_DIM = 72
FF = 3072
GRID = 16
eps_norm = 1e-06


def unpack_weights(weight_all, bias_all):
    flat = weight_all.reshape(-1)
    layouts = ((D, 3 * D), (D, D), (D, 2 * FF), (D, 6 * D), (FF, D))
    pieces = []
    offset = 0
    for layout in layouts:
        amount = layout[0] * layout[1]
        pieces.append(flat[offset : offset + amount].reshape(layout))
        offset = offset + amount
    offset = 0
    for amount in (3 * D, D, 2 * FF, 6 * D):
        pieces.append(bias_all[offset : offset + amount])
        offset = offset + amount
    return tuple(pieces)


def rope_tables():
    quarter = HEAD_DIM // 4
    places = jnp.arange(GRID * GRID, dtype=jnp.int32)
    rows_at = (places // GRID).astype(jnp.float32)
    cols_at = (places % GRID).astype(jnp.float32)
    freqs = 10000.0 ** (-jnp.arange(quarter, dtype=jnp.float32) / quarter)
    along_rows = rows_at[:, None] * freqs[None, :]
    along_cols = cols_at[:, None] * freqs[None, :]
    angles = jnp.concatenate([along_rows, along_rows, along_cols, along_cols], axis=1)
    return (jnp.cos(angles)[:, None, :], jnp.sin(angles)[:, None, :])


def turn_half(values):
    quarter = values.shape[-1] // 4
    first = values[..., :quarter]
    second = values[..., quarter : 2 * quarter]
    third = values[..., 2 * quarter : 3 * quarter]
    fourth = values[..., 3 * quarter :]
    return jnp.concatenate([-second, first, -fourth, third], axis=-1)


def norm_parts(values):
    centred = values - jnp.mean(values, -1, keepdims=True)
    inverse = lax.rsqrt(jnp.mean(centred * centred, -1, keepdims=True) + eps_norm)
    return (centred * inverse, inverse)


def norm_back(grad_normed, normed, inverse):
    return inverse * (
        grad_normed
        - jnp.mean(grad_normed, -1, keepdims=True)
        - normed * jnp.mean(grad_normed * normed, -1, keepdims=True)
    )


def rms_parts(values):
    inverse = lax.rsqrt(jnp.mean(values * values, -1, keepdims=True) + eps_norm)
    return (values * inverse, inverse)


def rms_back(grad_normed, normed, inverse):
    return inverse * (grad_normed - normed * jnp.mean(grad_normed * normed, -1, keepdims=True))


def on_device(tokens, conditions, cotangent, slot_mask, weight_flat, bias_flat):
    f32 = jnp.float32
    bf16 = jnp.bfloat16
    slots = conditions.shape[0]
    length = GRID * GRID
    rows_all = slots * length
    scale = 1.0 / math.sqrt(HEAD_DIM)
    heads_shape = (slots, length, HEADS, HEAD_DIM)
    weight_all, bias_all = (
        lax.all_gather(weight_flat, ("fsdp", "dp"), axis=0, tiled=True),
        lax.all_gather(bias_flat, ("fsdp", "dp"), axis=0, tiled=True),
    )
    (
        query_key_value_weight,
        projection_weight,
        feedforward_weight,
        w_ada,
        down_weight,
        query_key_value_bias,
        projection_bias,
        feedforward_bias,
        b_ada,
    ) = unpack_weights(weight_all, bias_all)
    cosines, sines = rope_tables()
    mask_f = slot_mask.astype(f32)[:, None, None]
    x_f = tokens.astype(f32).reshape(slots, length, D)
    cond_f = conditions.astype(f32)
    cond_act = jax.nn.silu(cond_f).astype(bf16)
    modulation = jnp.dot(cond_act, w_ada, preferred_element_type=f32) + b_ada.astype(f32)
    shift_a, scale_a, gate_a, shift_b, scale_b, gate_b = [
        modulation[:, None, place * D : (place + 1) * D] for place in range(6)
    ]
    normed_a, inv_a = norm_parts(x_f)
    attention_input = (normed_a * (1.0 + scale_a) + shift_a).astype(bf16).reshape(rows_all, D)
    projected_output = (
        jnp.dot(attention_input, query_key_value_weight, preferred_element_type=f32)
        + query_key_value_bias.astype(f32)
    ).reshape(slots, length, 3 * D)
    q_norm, inv_q = rms_parts(projected_output[..., :D].reshape(heads_shape))
    k_norm, inv_k = rms_parts(projected_output[..., D : 2 * D].reshape(heads_shape))
    queries = (q_norm * cosines + turn_half(q_norm) * sines).astype(bf16)
    keys = (k_norm * cosines + turn_half(k_norm) * sines).astype(bf16)
    values = projected_output[..., 2 * D :].reshape(heads_shape).astype(bf16)
    scores = jnp.einsum("slhe,smhe->shlm", queries, keys, preferred_element_type=f32) * scale
    row_max = jnp.max(scores, -1, keepdims=True)
    log_total = row_max + jnp.log(jnp.sum(jnp.exp(scores - row_max), -1, keepdims=True))
    probs_low = jnp.exp(scores - log_total).astype(bf16)
    attention_output = (
        jnp.einsum("shlm,smhe->slhe", probs_low, values, preferred_element_type=f32)
        .astype(bf16)
        .reshape(rows_all, D)
    )
    attention_branch = (
        jnp.dot(attention_output, projection_weight, preferred_element_type=f32)
        + projection_bias.astype(f32)
    ).reshape(slots, length, D)
    middle = x_f + gate_a * attention_branch
    normed_b, inv_b = norm_parts(middle)
    feedforward_input = (normed_b * (1.0 + scale_b) + shift_b).astype(bf16).reshape(rows_all, D)
    mixed_tokens = jnp.dot(
        feedforward_input, feedforward_weight, preferred_element_type=f32
    ) + feedforward_bias.astype(f32)
    gate_part = mixed_tokens[:, :FF]
    up_part = mixed_tokens[:, FF:]
    hidden_state = (jax.nn.silu(gate_part) * up_part).astype(bf16)
    feedforward_branch = jnp.dot(hidden_state, down_weight, preferred_element_type=f32).reshape(
        slots, length, D
    )
    out = ((middle + gate_b * feedforward_branch) * mask_f).astype(bf16).reshape(rows_all, D)
    weight_all, bias_all = (
        lax.all_gather(weight_flat, ("fsdp", "dp"), axis=0, tiled=True),
        lax.all_gather(bias_flat, ("fsdp", "dp"), axis=0, tiled=True),
    )
    (
        query_key_value_weight,
        projection_weight,
        feedforward_weight,
        w_ada,
        down_weight,
        query_key_value_bias,
        projection_bias,
        feedforward_bias,
        b_ada,
    ) = unpack_weights(weight_all, bias_all)
    g_out = cotangent.astype(f32).reshape(slots, length, D) * mask_f
    g_branch_b = (gate_b * g_out).astype(bf16).reshape(rows_all, D)
    g_gate_b = jnp.sum(g_out * feedforward_branch, axis=1)
    grad_down = jnp.einsum("rf,rd->fd", hidden_state, g_branch_b, preferred_element_type=f32)
    g_hidden = jnp.einsum("rd,fd->rf", g_branch_b, down_weight, preferred_element_type=f32)
    sigma_gate = jax.nn.sigmoid(gate_part)
    g_mixed = jnp.concatenate(
        [
            g_hidden * up_part * sigma_gate * (1.0 + gate_part * (1.0 - sigma_gate)),
            g_hidden * (gate_part * sigma_gate),
        ],
        axis=1,
    ).astype(bf16)
    grad_mlp = jnp.einsum("rd,rf->df", feedforward_input, g_mixed, preferred_element_type=f32)
    grad_b_mlp = jnp.sum(g_mixed.astype(f32), axis=0)
    g_input_b = jnp.einsum(
        "rf,df->rd", g_mixed, feedforward_weight, preferred_element_type=f32
    ).reshape(slots, length, D)
    g_shift_b = jnp.sum(g_input_b, axis=1)
    g_scale_b = jnp.sum(g_input_b * normed_b, axis=1)
    g_middle = g_out + norm_back(g_input_b * (1.0 + scale_b), normed_b, inv_b)
    g_branch_a = (gate_a * g_middle).astype(bf16).reshape(rows_all, D)
    g_gate_a = jnp.sum(g_middle * attention_branch, axis=1)
    grad_w_out = jnp.einsum("rd,re->de", attention_output, g_branch_a, preferred_element_type=f32)
    grad_b_out = jnp.sum(g_branch_a.astype(f32), axis=0)
    g_attended = (
        jnp.einsum("re,de->rd", g_branch_a, projection_weight, preferred_element_type=f32)
        .astype(bf16)
        .reshape(heads_shape)
    )
    scores = jnp.einsum("slhe,smhe->shlm", queries, keys, preferred_element_type=f32) * scale
    probs = jnp.exp(scores - log_total)
    probs_low = probs.astype(bf16)
    g_probs = jnp.einsum("slhe,smhe->shlm", g_attended, values, preferred_element_type=f32)
    g_values = jnp.einsum("shlm,slhe->smhe", probs_low, g_attended, preferred_element_type=f32)
    g_scores = (probs * (g_probs - jnp.sum(probs * g_probs, -1, keepdims=True))).astype(bf16)
    g_queries = jnp.einsum("shlm,smhe->slhe", g_scores, keys, preferred_element_type=f32) * scale
    g_keys = jnp.einsum("shlm,slhe->smhe", g_scores, queries, preferred_element_type=f32) * scale
    g_q = rms_back(g_queries * cosines - turn_half(g_queries) * sines, q_norm, inv_q)
    g_k = rms_back(g_keys * cosines - turn_half(g_keys) * sines, k_norm, inv_k)
    g_projected = jnp.concatenate(
        [g_q.reshape(rows_all, D), g_k.reshape(rows_all, D), g_values.reshape(rows_all, D)], axis=1
    ).astype(bf16)
    grad_qkv = jnp.einsum("rd,re->de", attention_input, g_projected, preferred_element_type=f32)
    grad_b_qkv = jnp.sum(g_projected.astype(f32), axis=0)
    g_input_a = jnp.einsum(
        "re,de->rd", g_projected, query_key_value_weight, preferred_element_type=f32
    ).reshape(slots, length, D)
    g_shift_a = jnp.sum(g_input_a, axis=1)
    g_scale_a = jnp.sum(g_input_a * normed_a, axis=1)
    grad_tokens = g_middle + norm_back(g_input_a * (1.0 + scale_a), normed_a, inv_a)
    g_modulation = jnp.concatenate(
        [g_shift_a, g_scale_a, g_gate_a, g_shift_b, g_scale_b, g_gate_b], axis=1
    ).astype(bf16)
    grad_ada = jnp.einsum("sd,se->de", cond_act, g_modulation, preferred_element_type=f32)
    grad_b_ada = jnp.sum(g_modulation.astype(f32), axis=0)
    g_cond = jnp.einsum("se,de->sd", g_modulation, w_ada, preferred_element_type=f32)
    sigma_cond = jax.nn.sigmoid(cond_f)
    grad_conditions = g_cond * sigma_cond * (1.0 + cond_f * (1.0 - sigma_cond))
    narrow_count = lax.axis_size("fsdp")
    wide_count = lax.axis_size("dp")
    grads_big = jnp.concatenate(
        [
            grad_qkv.reshape(-1),
            grad_w_out.reshape(-1),
            grad_mlp.reshape(-1),
            grad_ada.reshape(-1),
            grad_down.reshape(-1),
        ]
    ).reshape(narrow_count, wide_count, -1, 128)
    grads_small = jnp.concatenate([grad_b_qkv, grad_b_out, grad_b_mlp, grad_b_ada]).reshape(
        narrow_count, wide_count, -1
    )
    spread_big, spread_small = (
        lax.all_to_all(
            lax.all_to_all(
                grads_big.astype(jnp.bfloat16), "fsdp", split_axis=0, concat_axis=0, tiled=True
            ),
            "dp",
            split_axis=1,
            concat_axis=1,
            tiled=True,
        ).astype(grads_big.dtype),
        lax.all_to_all(
            lax.all_to_all(
                grads_small.astype(jnp.bfloat16), "fsdp", split_axis=0, concat_axis=0, tiled=True
            ),
            "dp",
            split_axis=1,
            concat_axis=1,
            tiled=True,
        ).astype(grads_small.dtype),
    )
    part_weights = jnp.sum(spread_big, axis=(0, 1))
    part_biases = jnp.sum(spread_small, axis=(0, 1))
    return (out, grad_tokens.reshape(rows_all, D), grad_conditions, part_weights, part_biases)


def solution(mesh):
    return jax.shard_map(
        on_device,
        mesh=mesh,
        in_specs=(
            P(("fsdp", "dp"), None),
            P(("fsdp", "dp"), None),
            P(("fsdp", "dp"), None),
            P(("fsdp", "dp")),
            P(("fsdp", "dp"), None),
            P(("fsdp", "dp")),
        ),
        out_specs=(
            P(("fsdp", "dp"), None),
            P(("fsdp", "dp"), None),
            P(("fsdp", "dp"), None),
            P(("fsdp", "dp"), None),
            P(("fsdp", "dp")),
        ),
        check_vma=False,
    )
```

profile of v0, /device:TPU:0, one launch (start us, length us, event | category | flops | bytes accessed | tf_op | source)
XLA Modules:
  0.0 2413.1 jit_solution(1016306333423830473)
XLA Ops:
  13.1 45.2 %all-reduce = bf16[17664]{0:T(1024)(128)(2,1)S(1)} all-reduce(bf16[17664]{0:T(1024)(128)(2,1)S(1)} %dynamic-update-slice), channel_id=1, replica_groups=mesh['fsdp'=4,'dp'=8] {'fsdp','dp'}, use_global_device_ids=true, to_apply=%add | all-reduce | flops 17664 | bytes 70656
  60.6 217.3 %all-gather.2.cloned.1.call-done = bf16[186624,128]{1,0:T(8,128)(2,1)} async-done(((bf16[5832,128]{1,0:T(8,128)(2,1)}), bf16[186624,128]{1,0:T(8,128)(2,1)}) %all-gather.2.cloned.1.call-update) | async-done | bytes 47775760 | tf_op jit(solution)/shard_map/all_gather | solution.py:84
  284.3 14.0 reshape.431
  298.3 14.0 reshape.415
  319.1 15.2 reshape.433
  334.3 15.2 reshape.407
  349.5 13.4 slice.155
  362.9 29.2 %reshape.406 = bf16[1152,6912]{1,0:T(8,128)(2,1)} reshape(bf16[62208,128]{1,0:T(8,128)(2,1)} %slice.155) | data formatting | bytes 31850496 | tf_op jit(solution)/shard_map/reshape | solution.py:22
  409.9 12.8 slice.178
  422.7 20.3 reshape.432
  443.0 20.3 reshape.414
  508.5 15.8 convolution_add_fusion
  524.2 13.0 multiply_convert_fusion.2
  551.4 17.1 multiply_reduce_fusion.3
  639.6 10.5 fusion
  681.0 13.6 reshape.428
  698.9 15.9 reshape.424
  714.8 13.9 copy.106
  728.7 30.9 %reshape.427 = bf16[7962624]{0:T(1024)(128)(2,1)} reshape(bf16[1152,6912]{1,0:T(8,128)(2,1)} %convolution_convert_fusion) | data formatting | bytes 31850496 | tf_op jit(solution)/shard_map/reshape | solution.py:225
  790.7 11.6 all-to-all-start
  802.9 514.4 %all-to-all-done = bf16[4,8,5832,128]{3,2,1,0:T(8,128)(2,1)} async-done(((bf16[4,8,5832,128]{3,2,1,0:T(8,128)(2,1)}), bf16[4,8,5832,128]{3,2,1,0:T(8,128)(2,1)}, u32[]{:S(2)}, u32[]{:S(2)}) %all-to-all-start) | async-done | bytes 47775776 | tf_op jit(solution)/shard_map/all_to_all | solution.py:234
  1320.7 32.0 %copy.93 = bf16[4,8,5832,128]{3,2,0,1:T(8,128)(2,1)} copy(bf16[4,8,5832,128]{3,2,1,0:T(8,128)(2,1)} %all-to-all-done) | data formatting | bytes 95551488 | tf_op jit(solution)/shard_map/all_to_all | solution.py:234
  1372.0 1017.0 %all-to-all-done.1 = bf16[4,8,5832,128]{3,2,0,1:T(8,128)(2,1)} async-done(((bf16[4,8,5832,128]{3,2,0,1:T(8,128)(2,1)}), bf16[4,8,5832,128]{3,2,0,1:T(8,128)(2,1)}, u32[]{:S(2)}, u32[]{:S(2)}) %all-to-all-start.1) | async-done | bytes 47775776 | tf_op jit(solution)/shard_map/all_to_all | solution.py:233
  2389.0 17.1 convert_reduce_fusion
  (290 shorter events, 258.1 us)
Async XLA Ops:
  7.2 270.7 %all-gather.2.cloned.1.call-start = ((), (), s32[]{:S(2)}) async-start(), calls=%async_computation.4 | async-start | bytes 49268736 | tf_op jit(solution)/shard_map/all_gather | solution.py:84
  362.9 29.2 %copy-start.55 = (bf16[2,1152]{1,0:T(2,128)(2,1)S(1)}, bf16[2,1152]{1,0:T(2,128)(2,1)}, u32[]{:S(2)}) copy-start(bf16[2,1152]{1,0:T(2,128)(2,1)} %param.7) | copy-start | bytes 13828
  392.1 9.2 copy-start.22
  508.4 15.8 copy-start.35
  508.4 15.8 copy-start.37
  508.5 34.1 %slice-start.8 = ((s8[7077888]{0:T(1024)(128)(4,1)}), s8[4194304]{0:T(1024)(128)(4,1)S(1)}, s32[]{:S(2)}) async-start(s8[7077888]{0:T(1024)(128)(4,1)} %bitcast.165), calls=%async_computation.13 | async-start | bytes 8388608
  524.2 18.3 slice-start.9
  596.9 10.6 slice-start
  602.3 9.7 copy-start.14
  639.6 10.5 copy-start.15
  655.6 9.4 copy-start.6
  655.6 9.4 copy-start.21
  655.6 9.4 copy-start.63
  655.6 9.4 copy-start.64
  681.0 13.6 copy-start.58
  681.0 13.6 copy-start.60
  695.4 95.3 %all-to-all-start.2 = ((bf16[4,8,552]{2,1,0:T(8,128)(2,1)}), bf16[4,8,552]{2,1,0:T(8,128)(2,1)S(1)}, u32[]{:S(2)}, u32[]{:S(2)}) async-start(bf16[4,8,552]{2,1,0:T(8,128)(2,1)} %convert_element_type.155), calls=%async_computation.2 | async-start | bytes 81920 | tf_op jit(solution)/shard_map/all_to_all | solution.py:243
  759.6 11.3 copy-start.4
  766.8 11.2 slice-start.2
  770.9 9.6 slice-start.5
  770.9 16.4 slice-start.6
  790.7 526.7 %all-to-all-start = ((bf16[4,8,5832,128]{3,2,1,0:T(8,128)(2,1)}), bf16[4,8,5832,128]{3,2,1,0:T(8,128)(2,1)}, u32[]{:S(2)}, u32[]{:S(2)}) async-start(bf16[4,8,5832,128]{3,2,1,0:T(8,128)(2,1)} %bitcast.151), calls=%async_computation | async-start | bytes 95551488 | tf_op jit(solution)/shard_map/all_to_all | solution.py:234
  1317.4 35.3 %all-to-all-start.3 = ((bf16[4,8,552]{2,0,1:T(4,128)(2,1)}), bf16[4,8,552]{2,0,1:T(4,128)(2,1)S(1)}, u32[]{:S(2)}, u32[]{:S(2)}) async-start(bf16[4,8,552]{2,0,1:T(4,128)(2,1)} %copy.94), calls=%async_computation.3 | async-start | bytes 81920 | tf_op jit(solution)/shard_map/all_to_all | solution.py:242
  1352.7 1036.3 %all-to-all-start.1 = ((bf16[4,8,5832,128]{3,2,0,1:T(8,128)(2,1)}), bf16[4,8,5832,128]{3,2,0,1:T(8,128)(2,1)}, u32[]{:S(2)}, u32[]{:S(2)}) async-start(bf16[4,8,5832,128]{3,2,0,1:T(8,128)(2,1)} %copy.93), calls=%async_computation.1 | async-start | bytes 95551488 | tf_op jit(solution)/shard_map/all_to_all | solution.py:233
  (64 other events, 237.0 us)
Sparse Core Ops, SparseCore 0:
  10.9 267.0 all-gather.1
where the time goes:
time: 2420 us; the launch traced here: 2410 us
  waiting for transfers between devices  1750 us (72%)
  local copies, waits for them, and re-layouts  367 us (15%)
  matrix products  146 us (6%)
  other arithmetic  63.7 us (3%)
  blocking collectives  45.2 us (2%)
  starting transfers between devices  26.8 us (1%)
    all_to_all x1, waiting for transfers between devices, on_device(): lax.all_to_all(lax.all_to_all(grads_big.astype(jnp.bfloat16), 'fsdp', spl...  1020 us
    all_to_all x1, waiting for transfers between devices, on_device(): lax.all_to_all(grads_big.astype(jnp.bfloat16), 'fsdp', split_axis=0, conc...  514 us
    all_gather x1, waiting for transfers between devices, on_device(): lax.all_gather(weight_flat, ('fsdp', 'dp'), axis=0, tiled=True)  217 us
    reshape x8, local copies, waits for them, and re-layouts, unpack_weights(): pieces.append(flat[offset:offset + amount].reshape(layout))  134 us
    unnamed x186, local copies, waits for them, and re-layouts  52.7 us
  transfers between devices with their start and end apart: 5, of which 3 were waited for; matrix products, arithmetic and copies ran while one was open for 6% of the time, Pallas kernels for 0%

commit v1 on v0

--- a/solution.py
+++ b/solution.py
@@ -10,6 +10,28 @@
 FF = 3072
 GRID = 16
 eps_norm = 1e-06
+
+
+def in_order(blocks, dim):
+    lengths = list(blocks.shape[1:])
+    lengths[dim] *= blocks.shape[0]
+    return jnp.moveaxis(blocks, 0, dim).reshape(lengths)
+
+
+def grow_blocks(x, axis):
+    size = lax.axis_size(axis)
+    tiles = x[None]
+    for level in range(size.bit_length() - 1):
+        bit = 1 << level
+        theirs = lax.ppermute(tiles, axis, [(i, i ^ bit) for i in range(size)])
+        both = jnp.stack([tiles, theirs])
+        upper = lax.axis_index(axis) >> level & 1
+        tiles = jnp.where(upper == 0, both, both[::-1]).reshape(-1, *x.shape)
+    return tiles
+
+
+def gather_by_bits(value, axis, dim):
+    return in_order(grow_blocks(value, axis), dim)
 
 
 def unpack_weights(weight_all, bias_all):
@@ -81,7 +103,7 @@
     scale = 1.0 / math.sqrt(HEAD_DIM)
     heads_shape = (slots, length, HEADS, HEAD_DIM)
     weight_all, bias_all = (
-        lax.all_gather(weight_flat, ("fsdp", "dp"), axis=0, tiled=True),
+        gather_by_bits(weight_flat, ("fsdp", "dp"), 0),
         lax.all_gather(bias_flat, ("fsdp", "dp"), axis=0, tiled=True),
     )
     (

time: 2420 us -> 3880 us (1.60)
  waiting for transfers between devices: 1750 us -> 2280 us
  blocking collectives: 45.2 us -> 540 us
  local copies, waits for them, and re-layouts: 367 us -> 651 us
  other arithmetic: 63.7 us -> 185 us
    ppermute x0 -> x5, waiting for transfers between devices: none -> 787 us  [grow_blocks(): theirs = lax.ppermute(tiles, axis, [(i, i ^ bit) for i in range(size)])]
    unnamed x1, blocking collectives: 45.2 us -> 540 us
    slice x5 -> x9, local copies, waits for them, and re-layouts: 42.3 us -> 364 us  [unpack_weights(): pieces.append(flat[offset:offset + amount].reshape(layout))]
    all_gather x1, waiting for transfers between devices: 217 us -> 0.01 us  [on_device(): lax.all_gather(weight_flat, ('fsdp', 'dp'), axis=0, tiled=True)]
    select_n x0 -> x4, other arithmetic: none -> 68.1 us  [grow_blocks(): tiles = jnp.where(upper == 0, both, both[::-1]).reshape(-1, *x.shape)]
    another operation x1 -> x7, other arithmetic: 3.16 us -> 58.5 us  [the longest x6 54.5 us: grow_blocks(): both = jnp.stack([tiles, theirs])]
    reshape x8 -> x5, local copies, waits for them, and re-layouts: 134 us -> 84.8 us  [unpack_weights(): pieces.append(flat[offset:offset + amount].reshape(layout))]
    all_to_all x1, waiting for transfers between devices: 1020 us -> 975 us  [on_device(): lax.all_to_all(lax.all_to_all(grads_big.astype(jnp.bfloat16), 'fsdp', spl...]
  transfers between devices with their start and end apart: 5 -> 10, of which waited for: 3 -> 6; matrix products, arithmetic and copies ran while one was open for 6% -> 16% of each run, Pallas kernels for 0% -> 0%
where the time goes in v1:
time: 3880 us; the launch traced here: 3870 us
  waiting for transfers between devices  2280 us (59%)
  local copies, waits for them, and re-layouts  651 us (17%)
  blocking collectives  540 us (14%)
  other arithmetic  185 us (5%)
  matrix products  159 us (4%)
  starting transfers between devices  39.7 us (1%)
    all_to_all x1, waiting for transfers between devices, on_device(): lax.all_to_all(lax.all_to_all(grads_big.astype(jnp.bfloat16), 'fsdp', spl...  975 us
    ppermute x5, waiting for transfers between devices, grow_blocks(): theirs = lax.ppermute(tiles, axis, [(i, i ^ bit) for i in range(size)])  787 us
    unnamed x1, blocking collectives  540 us
    all_to_all x1, waiting for transfers between devices, on_device(): lax.all_to_all(grads_big.astype(jnp.bfloat16), 'fsdp', split_axis=0, conc...  513 us
    slice x9, local copies, waits for them, and re-layouts, unpack_weights(): pieces.append(flat[offset:offset + amount].reshape(layout))  364 us
    reshape x5, local copies, waits for them, and re-layouts, unpack_weights(): pieces.append(flat[offset:offset + amount].reshape(layout))  84.8 us
  transfers between devices with their start and end apart: 10, of which 6 were waited for; matrix products, arithmetic and copies ran while one was open for 16% of the time, Pallas kernels for 0%

profile of v1, /device:TPU:0, one launch (start us, length us, event | category | flops | bytes accessed | tf_op | source)
XLA Modules:
  0.0 3865.4 jit_solution(15305956656096616226)
XLA Ops:
  17.2 142.9 %collective-permute-done.1 = bf16[2,5832,128]{2,1,0:T(8,128)(2,1)} collective-permute-done((bf16[2,5832,128]{2,1,0:T(8,128)(2,1)}, bf16[2,5832,128]{2,1,0:T(8,128)(2,1)}, u32[]{:S(2)}, u32[]{:S(2)}) %collective-permute-start.1) | collective-permute-done | bytes 2986016 | tf_op jit(solution)/shard_map/ppermute | solution.py:26
  172.4 385.5 %collective-permute-done.2 = bf16[4,5832,128]{2,1,0:T(8,128)(2,1)} collective-permute-done((bf16[4,5832,128]{2,1,0:T(8,128)(2,1)}, bf16[4,5832,128]{2,1,0:T(8,128)(2,1)}, u32[]{:S(2)}, u32[]{:S(2)}) %collective-permute-start.2) | collective-permute-done | bytes 5972000 | tf_op jit(solution)/shard_map/ppermute | solution.py:26
  571.6 255.5 %collective-permute-done.3 = bf16[8,5832,128]{2,1,0:T(8,128)(2,1)} collective-permute-done((bf16[8,5832,128]{2,1,0:T(8,128)(2,1)}, bf16[8,5832,128]{2,1,0:T(8,128)(2,1)}, u32[]{:S(2)}, u32[]{:S(2)}) %collective-permute-start.3) | collective-permute-done | bytes 11943968 | tf_op jit(solution)/shard_map/ppermute | solution.py:26
  854.5 540.5 %all-reduce = bf16[17664]{0:T(1024)(128)(2,1)S(1)} all-reduce(bf16[17664]{0:T(1024)(128)(2,1)S(1)} %dynamic-update-slice), channel_id=1, replica_groups=mesh['fsdp'=4,'dp'=8] {'fsdp','dp'}, use_global_device_ids=true, to_apply=%add | all-reduce | flops 17664 | bytes 70656
  1398.5 31.9 pad_maximum_fusion
  1430.4 46.6 %reverse_select_fusion = bf16[2,16,5832,128]{3,2,1,0:T(8,128)(2,1)} fusion(bf16[2,16,5832,128]{3,2,1,0:T(8,128)(2,1)} %pad_maximum_fusion, pred[]{:T(512)S(6)} %eq.17), kind=kLoop, calls=%fused_computation.1 | loop fusion | flops 23887872 | bytes 95551488 | tf_op jit(solution)/shard_map/jit(_where)/select_n | solution.py:29
  1477.1 84.3 %slice.142 = bf16[3456,6912]{1,0:T(8,128)(2,1)} reshape(bf16[2,16,5832,128]{3,2,1,0:T(8,128)(2,1)} %reverse_select_fusion) | data formatting | bytes 95551488 | tf_op jit(solution)/shard_map/slice | solution.py:44
  1561.4 84.6 %slice.148 = bf16[6912,3456]{1,0:T(8,128)(2,1)} reshape(bf16[2,16,5832,128]{3,2,1,0:T(8,128)(2,1)} %reverse_select_fusion) | data formatting | bytes 95551488 | tf_op jit(solution)/shard_map/slice | solution.py:44
  1645.9 87.3 %slice.162 = bf16[20736,1152]{1,0:T(8,128)(2,1)} reshape(bf16[2,16,5832,128]{3,2,1,0:T(8,128)(2,1)} %reverse_select_fusion) | data formatting | bytes 95551488 | tf_op jit(solution)/shard_map/slice | solution.py:44
  1733.3 65.4 %slice.168 = bf16[3888,6144]{1,0:T(8,128)(2,1)} reshape(bf16[2,16,5832,128]{3,2,1,0:T(8,128)(2,1)} %reverse_select_fusion) | data formatting | bytes 95551488 | tf_op jit(solution)/shard_map/slice | solution.py:44
  1855.6 14.8 fusion.4
  1876.7 14.0 reshape.438
  1903.5 20.3 reshape.457
  1948.2 17.1 multiply_reduce_fusion.3
  2047.2 15.2 reshape.458
  2127.7 15.9 reshape.449
  2155.3 14.0 copy.106
  2169.3 30.9 reshape.452
  2200.2 13.9 reshape.453
  2256.5 513.0 %all-to-all-done = bf16[4,8,5832,128]{3,2,1,0:T(8,128)(2,1)} async-done(((bf16[4,8,5832,128]{3,2,1,0:T(8,128)(2,1)}), bf16[4,8,5832,128]{3,2,1,0:T(8,128)(2,1)}, u32[]{:S(2)}, u32[]{:S(2)}) %all-to-all-start) | async-done | bytes 47775776 | tf_op jit(solution)/shard_map/all_to_all | solution.py:256
  2773.0 31.9 copy.93
  2826.6 29.0 reshape.445
  2866.6 974.6 %all-to-all-done.1 = bf16[4,8,5832,128]{3,2,0,1:T(8,128)(2,1)} async-done(((bf16[4,8,5832,128]{3,2,0,1:T(8,128)(2,1)}), bf16[4,8,5832,128]{3,2,0,1:T(8,128)(2,1)}, u32[]{:S(2)}, u32[]{:S(2)}) %all-to-all-start.1) | async-done | bytes 47775776 | tf_op jit(solution)/shard_map/all_to_all | solution.py:255
  3841.2 17.1 convert_reduce_fusion
  (317 shorter events, 403.9 us)
Async XLA Ops:
  7.2 1863.2 %all-gather.2.cloned.1.call-start = ((), (), s32[]{:S(2)}) async-start(), calls=%async_computation.4 | async-start | bytes 49268736 | tf_op jit(solution)/shard_map/all_gather | solution.py:167
  7.9 3.7 collective-permute-start
  14.2 145.8 %collective-permute-start.1 = (bf16[2,5832,128]{2,1,0:T(8,128)(2,1)}, bf16[2,5832,128]{2,1,0:T(8,128)(2,1)}, u32[]{:S(2)}, u32[]{:S(2)}) collective-permute-start(bf16[2,5832,128]{2,1,0:T(8,128)(2,1)} %get-tuple-element.26), channel_id=1, source_target_pairs={{0,2},{1,3},{2,0},{3,1},{4,6},{5,7},{6,4},{7,5},{8,10},{9,11},{10,... | collective-permute-start | bytes 8957960 | tf_op jit(solution)/shard_map/ppermute | solution.py:26
  166.2 391.7 %collective-permute-start.2 = (bf16[4,5832,128]{2,1,0:T(8,128)(2,1)}, bf16[4,5832,128]{2,1,0:T(8,128)(2,1)}, u32[]{:S(2)}, u32[]{:S(2)}) collective-permute-start(bf16[4,5832,128]{2,1,0:T(8,128)(2,1)} %bitcast.8), channel_id=1, source_target_pairs={{0,4},{1,5},{2,6},{3,7},{4,0},{5,1},{6,2},{7,3},{8,12},{9,13},{10,... | collective-permute-start | bytes 17915912 | tf_op jit(solution)/shard_map/ppermute | solution.py:26
  570.1 257.0 %collective-permute-start.3 = (bf16[8,5832,128]{2,1,0:T(8,128)(2,1)}, bf16[8,5832,128]{2,1,0:T(8,128)(2,1)}, u32[]{:S(2)}, u32[]{:S(2)}) collective-permute-start(bf16[8,5832,128]{2,1,0:T(8,128)(2,1)} %bitcast.11), channel_id=1, source_target_pairs={{0,8},{1,9},{2,10},{3,11},{4,12},{5,13},{6,14},{7,15},{8,0},{9,1},... | collective-permute-start | bytes 35831816 | tf_op jit(solution)/shard_map/ppermute | solution.py:26
  838.6 13.8 copy-start.5
  850.2 548.3 %collective-permute-start.4 = (bf16[16,5832,128]{2,1,0:T(8,128)(2,1)}, bf16[16,5832,128]{2,1,0:T(8,128)(2,1)}, u32[]{:S(2)}, u32[]{:S(2)}) collective-permute-start(bf16[16,5832,128]{2,1,0:T(8,128)(2,1)} %bitcast.14), channel_id=1, source_target_pairs={{0,16},{1,17},{2,18},{3,19},{4,20},{5,21},{6,22},{7,23},{8,24},{9,... | collective-permute-start | bytes 71663624 | tf_op jit(solution)/shard_map/ppermute | solution.py:26
  852.7 577.7 %copy-start.60 = (f32[512]{0:T(512)}, f32[512]{0:T(512)S(1)}, u32[]{:S(2)}) copy-start(f32[512]{0:T(512)S(1)} %broadcast_multiply_fusion.12) | copy-start | bytes 6148
  1733.3 65.4 %copy-start.49 = (f32[6912]{0:T(1024)S(1)}, f32[6912]{0:T(1024)}, u32[]{:S(2)}) copy-start(f32[6912]{0:T(1024)} %slice_convert_fusion.1) | copy-start | bytes 82948
  1733.3 65.4 %copy-start.52 = (bf16[2,1152]{1,0:T(2,128)(2,1)S(1)}, bf16[2,1152]{1,0:T(2,128)(2,1)}, u32[]{:S(2)}) copy-start(bf16[2,1152]{1,0:T(2,128)(2,1)} %param.7) | copy-start | bytes 13828
  1923.8 13.3 copy-start.57
  1923.8 13.3 copy-start.75
  2200.2 13.9 copy-start.55
  2200.2 13.9 copy-start.58
  2200.2 13.9 copy-start.65
  2214.8 29.5 all-to-all-start.2
  2218.4 14.8 slice-start.2
  2220.0 14.4 slice-start.5
  2220.1 21.0 slice-start.6
  2244.3 525.2 %all-to-all-start = ((bf16[4,8,5832,128]{3,2,1,0:T(8,128)(2,1)}), bf16[4,8,5832,128]{3,2,1,0:T(8,128)(2,1)}, u32[]{:S(2)}, u32[]{:S(2)}) async-start(bf16[4,8,5832,128]{3,2,1,0:T(8,128)(2,1)} %bitcast.176), calls=%async_computation | async-start | bytes 95551488 | tf_op jit(solution)/shard_map/all_to_all | solution.py:256
  2769.5 35.4 all-to-all-start.3
  2804.9 1036.3 %all-to-all-start.1 = ((bf16[4,8,5832,128]{3,2,0,1:T(8,128)(2,1)}), bf16[4,8,5832,128]{3,2,0,1:T(8,128)(2,1)}, u32[]{:S(2)}, u32[]{:S(2)}) async-start(bf16[4,8,5832,128]{3,2,0,1:T(8,128)(2,1)} %copy.93), calls=%async_computation.1 | async-start | bytes 95551488 | tf_op jit(solution)/shard_map/all_to_all | solution.py:255
  2826.6 29.1 copy-start.48
  2826.6 29.1 copy-start.54
  (73 other events, 351.4 us)
Sparse Core Ops, SparseCore 0:
  10.9 494.6 all-gather.1
